TPU v7x, 256 devices: a whole 4x4x8 slice. The times are simulated.
256 devices in a mesh: row: 4 (over x), col: 16 (over y_hi, z), pair: 4 (over y_lo, core).
Axes of the slice: x: 4, y: 4 (y_hi: 2, y_lo: 2; y = y_hi * 2 + y_lo), z: 8, core: 2. Of those that a mesh axis runs over, the one named last changes fastest.
Arguments:
- frames: bfloat16 [4, 2, 64, 512, 256], P('pair', None, 'row', 'col'), may hold values from -6 to 6
- offsets: int32 [4, 2, 16, 2], P('pair'), may hold values from -8 to 8, as said below
- weight: bfloat16 [3, 3, 256, 256], replicated, may hold values from -0.125 to 0.125
- bias: float32 [256], replicated, may hold values from -3 to 3
- cotangent: bfloat16 [4, 81, 64, 512], P('pair', None, 'row', 'col'), may hold values from -0.023925781 to 0.023925781
Outputs:
- corr: bfloat16 [4, 81, 64, 512], P('pair', None, 'row', 'col')
- grad_weight: float32 [3, 3, 256, 256], replicated
- grad_bias: float32 [256], replicated
Inputs may be any that keep to these rules, and one draw needn't show every extreme that they name: `offsets`: entry [.., 0] shifts rows and [.., 1] columns of one 32 x 32 block; both ends of the range occur in every draw.
All inputs are finite; a program needn't handle non-finite values.
Results may differ from a plain program's by a relative error of at most 0.0046.
Values may be sent and summed in bfloat16 or wider, within the bound.
No kernel may reach another device: no remote copies, remote signals or barrier semaphores. Data moves between devices by JAX's collectives and lax.ppermute only.
A program may use at most 64 MiB of HBM per device.

v0:
```python
import jax
import jax.numpy as jnp
from jax import lax
from jax.sharding import PartitionSpec as P

BLK = 32
RAD = 4
MAXOFF = 8


def with_halo(cells, sides, width):
    for axis, dim in sides:
        count = lax.axis_size(axis)
        ends = count - 1
        head = lax.slice_in_dim(cells, 0, width, axis=dim)
        tail = lax.slice_in_dim(cells, cells.shape[dim] - width, cells.shape[dim], axis=dim)
        cells = jnp.concatenate(
            [
                lax.ppermute(tail, axis, [(i, (i + 1) % count) for i in range(ends)]),
                cells,
                lax.ppermute(head, axis, [((i + 1) % count, i) for i in range(ends)]),
            ],
            axis=dim,
        )
    return cells


def band_take(scores):
    row_count, col_count, patch_width = scores.shape
    widened = jnp.pad(scores, ((0, 0), (0, 0), (0, 1)))
    flattened = widened.reshape(row_count, col_count * (patch_width + 1))
    flattened = jnp.pad(flattened, ((0, 0), (0, col_count)))
    return flattened.reshape(row_count, col_count, patch_width + 2)[:, :, : 2 * RAD + 1]


def band_spread(bands, patch_width):
    row_count, col_count, window_size = bands.shape
    widened = jnp.pad(bands, ((0, 0), (0, 0), (0, patch_width + 2 - window_size)))
    flattened = widened.reshape(row_count, col_count * (patch_width + 2))[
        :, : col_count * (patch_width + 1)
    ]
    return flattened.reshape(row_count, col_count, patch_width + 1)[:, :, :patch_width]


def block_scores(block_one, window_two):
    row_count, col_count = (block_one.shape[0], block_one.shape[1])
    window_size = 2 * RAD + 1
    score_list = []
    for row_shift in range(window_size):
        scores = jnp.einsum(
            "yxc,yzc->yxz",
            block_one,
            window_two[row_shift : row_shift + row_count],
            preferred_element_type=jnp.float32,
        )
        score_list.append(band_take(scores))
    stacked = jnp.stack(score_list)
    return jnp.transpose(stacked, (0, 3, 1, 2)).reshape(
        window_size * window_size, row_count, col_count
    )


def block_grads(cot_block, block_one, window_two):
    row_count, col_count, channels = block_one.shape
    window_size = 2 * RAD + 1
    patch_width = col_count + 2 * RAD
    cot_grid = jnp.transpose(
        cot_block.reshape(window_size, window_size, row_count, col_count), (0, 2, 3, 1)
    )
    grad_block = jnp.zeros((row_count, col_count, channels), jnp.float32)
    grad_window = jnp.zeros((row_count + 2 * RAD, patch_width, channels), jnp.float32)
    for row_shift in range(window_size):
        spread = band_spread(cot_grid[row_shift], patch_width)
        grad_block = grad_block + jnp.einsum(
            "yxz,yzc->yxc",
            spread,
            window_two[row_shift : row_shift + row_count],
            preferred_element_type=jnp.float32,
        )
        patch_term = jnp.einsum(
            "yxz,yxc->yzc", spread, block_one, preferred_element_type=jnp.float32
        )
        grad_window = grad_window.at[row_shift : row_shift + row_count].add(patch_term)
    return (grad_block, grad_window)


def convolve(padded, weight, bias, row_count, col_count):
    channels = weight.shape[3]
    accumulated = jnp.zeros((row_count * col_count, channels), jnp.float32)
    for tap_row in range(3):
        for tap_col in range(3):
            window = padded[tap_row : tap_row + row_count, tap_col : tap_col + col_count].reshape(
                row_count * col_count, -1
            )
            accumulated = accumulated + jnp.dot(
                window, weight[tap_row, tap_col], preferred_element_type=jnp.float32
            )
    return accumulated.reshape(row_count, col_count, channels) + bias


def weight_terms(padded, delta, input_float):
    row_count, col_count, channels = delta.shape
    flat_delta = delta.reshape(row_count * col_count, channels)
    tap_list = []
    for tap_row in range(3):
        for tap_col in range(3):
            window = padded[tap_row : tap_row + row_count, tap_col : tap_col + col_count].reshape(
                row_count * col_count, -1
            )
            if input_float:
                tap_list.append(
                    jnp.einsum(
                        "pc,pd->cd",
                        window.astype(jnp.float32),
                        flat_delta,
                        precision=lax.Precision.HIGHEST,
                    )
                )
            else:
                tap_list.append(
                    jnp.einsum("pc,pd->cd", window, flat_delta, preferred_element_type=jnp.float32)
                )
    return jnp.stack(tap_list).reshape(3, 3, channels, channels)


def shards(frames, offsets, weight, bias, cotangent):
    tile_rows, tile_cols, channels = (frames.shape[2], frames.shape[3], frames.shape[4])
    border_width = MAXOFF + RAD
    row_start = lax.axis_index("row") * tile_rows
    col_start = lax.axis_index("col") * tile_cols
    inv_root = channels ** (-0.5)
    bordered = with_halo(frames, (("row", 2), ("col", 3)), 1)
    first_pad = bordered[0, 0]
    second_pad = bordered[0, 1]
    pre_one = convolve(first_pad, weight, bias, tile_rows, tile_cols)
    pre_two = convolve(second_pad, weight, bias, tile_rows, tile_cols)
    feat_two = jnp.maximum(pre_two, 0.0).astype(jnp.bfloat16)
    padded_two = with_halo(feat_two, (("row", 0), ("col", 1)), border_width)
    feat_one = jnp.maximum(pre_one, 0.0).astype(jnp.bfloat16)
    sub_rows = min(tile_rows, BLK)
    gradient_second_padded = jnp.zeros(
        (tile_rows + 2 * border_width, tile_cols + 2 * border_width, channels), jnp.float32
    )
    zero_index = jnp.zeros((), jnp.int32)
    block_row = (row_start + 0) // BLK
    block_col = (col_start + 0) // BLK
    shift_pair = offsets[0, block_row, block_col]
    start = (0 + shift_pair[0] + MAXOFF, 0 + shift_pair[1] + MAXOFF, zero_index)
    window_two = lax.dynamic_slice(padded_two, start, (sub_rows + 2 * RAD, BLK + 2 * RAD, channels))
    corr_pieces = block_scores(feat_one, window_two) * inv_root
    cot_block = cotangent[0, :, 0:sub_rows, 0:BLK]
    grad_block, grad_window = block_grads(cot_block, feat_one, window_two)
    grad_pieces = grad_block * inv_root
    gradient_second_padded = lax.dynamic_update_slice(
        gradient_second_padded, grad_window * inv_root, start
    )
    corr = corr_pieces.astype(jnp.bfloat16)[None]
    carried_state = jnp.concatenate(
        [gradient_second_padded[:border_width], gradient_second_padded[-border_width:]], axis=0
    )
    incoming_block = with_halo(
        carried_state.astype(jnp.bfloat16), (("row", 0),), border_width
    ).astype(carried_state.dtype)
    central_index = gradient_second_padded[border_width : border_width + tile_rows]
    central_index = central_index.at[:border_width].add(incoming_block[:border_width])
    central_index = central_index.at[tile_rows - border_width :].add(
        incoming_block[3 * border_width :]
    )
    carried_state = jnp.concatenate(
        [central_index[:, :border_width], central_index[:, -border_width:]], axis=1
    )
    incoming_block = with_halo(
        carried_state.astype(jnp.bfloat16), (("col", 1),), border_width
    ).astype(carried_state.dtype)
    center = central_index[:, border_width : border_width + tile_cols]
    center = center.at[:, :border_width].add(incoming_block[:, :border_width])
    center = center.at[:, tile_cols - border_width :].add(incoming_block[:, 3 * border_width :])
    delta_two = jnp.where(pre_two > 0, center, 0.0)
    delta_one = jnp.where(pre_one > 0, grad_pieces, 0.0).astype(jnp.bfloat16)
    grad_w = weight_terms(first_pad, delta_one, False) + weight_terms(second_pad, delta_two, True)
    grad_b = jnp.sum(delta_one.astype(jnp.float32), axis=(0, 1)) + jnp.sum(delta_two, axis=(0, 1))
    grad_w, grad_b = lax.psum((grad_w, grad_b), ("row", "col", "pair"))
    return (corr, grad_w, grad_b)


def solution(mesh):
    return jax.shard_map(
        shards,
        mesh=mesh,
        in_specs=(
            P("pair", None, "row", "col", None),
            P("pair", None, None, None),
            P(),
            P(),
            P("pair", None, "row", "col"),
        ),
        out_specs=(P("pair", None, "row", "col"), P(), P()),
        check_vma=False,
    )
```

profile of v0, /device:TPU:2, one launch (start us, length us, event | category | flops | bytes accessed | tf_op | source)
XLA Modules:
  0.0 393.6 jit_solution(6452110076248892458)
XLA Ops:
  7.2 0.8 fusion.142
  8.0 3.4 collective-permute-start
  11.4 2.4 collective-permute-start.1
  13.9 1.2 copy.31
  15.3 1.1 constant_dynamic-update-slice_fusion.1
  16.3 0.9 collective-permute-done.1
  17.3 3.8 collective-permute-start.2
  21.1 1.3 collective-permute-start.3
  22.4 0.5 fusion.147
  23.4 0.3 reshape.635
  24.2 0.3 reshape.637
  25.0 0.3 reshape.639
  25.8 0.3 reshape.641
  26.6 0.3 reshape.643
  27.4 0.3 reshape.645
  28.2 0.3 reshape.647
  29.0 0.3 reshape.649
  29.8 0.3 reshape.651
  32.8 0.4 pad_maximum_fusion
  33.3 1.6 fusion.144
  35.0 1.1 fusion.79
  38.2 0.7 copy-done.1
  40.0 0.3 fusion.5
  40.3 0.3 fusion.4
  40.7 0.3 fusion.3
  41.0 0.3 fusion.2
  41.3 0.3 fusion.1
  42.0 1.0 broadcast_multiply_fusion
  43.1 9.8 %dynamic_update_slice.3 = f32[40,56,256]{2,1,0:T(8,128)S(1)} dynamic-update-slice(f32[40,56,256]{2,1,0:T(8,128)S(1)} %broadcast_in_dim.4, f32[24,40,256]{2,1,0:T(8,128)} %broadcast_multiply_fusion, s32[]{:T(128)S(6)} %select_n.33, s32[]{:T(128)S(6)} %select_n.34, s32[]{:T(128)} %constant.386.clone.1) | dynamic-update-slice | bytes 1966084 | tf_op jit(solution)/shard_map/dynamic_update_slice | solution.py:154
  53.2 3.0 collective-permute-start.8
  56.2 3.2 collective-permute-start.9
  61.2 0.4 copy-done.24
  61.8 1.3 collective-permute-done.8
  63.1 2.4 collective-permute-done.9
  65.9 5.4 %collective-permute-start.10 = (bf16[16,12,256]{2,1,0:T(8,128)(2,1)S(1)}, bf16[16,12,256]{2,1,0:T(8,128)(2,1)S(1)}, u32[]{:S(2)}, u32[]{:S(2)}) collective-permute-start(bf16[16,12,256]{2,1,0:T(8,128)(2,1)S(1)} %get-tuple-element.181), channel_id=1, source_target_pairs={{0,4},{4,8},{8,12},{12,16},{16,20},{20,24},{24,28},{28,32},{32,36}... | collective-permute-start | bytes 294920 | tf_op jit(solution)/shard_map/ppermute | solution.py:19
  71.3 1.3 collective-permute-start.11
  72.9 0.9 collective-permute-done.10
  73.8 4.4 %collective-permute-done.11 = bf16[16,12,256]{2,1,0:T(8,128)(2,1)S(1)} collective-permute-done((bf16[16,12,256]{2,1,0:T(8,128)(2,1)S(1)}, bf16[16,12,256]{2,1,0:T(8,128)(2,1)S(1)}, u32[]{:S(2)}, u32[]{:S(2)}) %collective-permute-start.11) | collective-permute-done | bytes 98336 | tf_op jit(solution)/shard_map/ppermute | solution.py:21
  78.2 0.4 scatter-add.61
  78.7 0.3 scatter-add.64
  79.2 3.1 collective-permute-start.4
  82.3 2.8 collective-permute-start.5
  85.1 0.5 fusion.19
  85.6 0.5 fusion.18
  86.1 0.5 fusion.17
  86.6 0.5 fusion.16
  87.1 0.5 fusion.15
  87.6 0.5 fusion.14
  88.1 0.5 fusion.13
  88.6 0.5 fusion.12
  89.1 0.8 collective-permute-done.5
  90.1 4.7 %collective-permute-start.6 = (bf16[40,12,256]{2,1,0:T(8,128)(2,1)S(1)}, bf16[40,12,256]{2,1,0:T(8,128)(2,1)S(1)}, u32[]{:S(2)}, u32[]{:S(2)}) collective-permute-start(bf16[40,12,256]{2,1,0:T(8,128)(2,1)S(1)} %get-tuple-element.175), channel_id=1, source_target_pairs={{0,4},{4,8},{8,12},{12,16},{16,20},{20,24},{24,28},{28,32},{32,36}... | collective-permute-start | bytes 737288 | tf_op jit(solution)/shard_map/ppermute | solution.py:19
  94.8 1.3 collective-permute-start.7
  96.1 0.5 fusion.11
  96.6 2.7 collective-permute-done.6
  99.4 5.5 %collective-permute-done.7 = bf16[40,12,256]{2,1,0:T(8,128)(2,1)S(1)} collective-permute-done((bf16[40,12,256]{2,1,0:T(8,128)(2,1)S(1)}, bf16[40,12,256]{2,1,0:T(8,128)(2,1)S(1)}, u32[]{:S(2)}, u32[]{:S(2)}) %collective-permute-start.7) | collective-permute-done | bytes 245792 | tf_op jit(solution)/shard_map/ppermute | solution.py:21
  104.8 1.4 fusion.32
  106.4 0.9 fusion.39
  114.2 1.7 add.331
  115.9 0.9 copy-done.22
  123.5 1.0 copy.41
  124.5 82.2 %psum.15 = f32[256]{0:T(256)} all-reduce(f32[256]{0:T(256)S(1)} %add.333), channel_id=1, replica_groups=mesh['row'=4,'col'=16,'pair'=4] {'row','col','pair'}, use_global_device_ids=true, to_apply=%region_3.4 | all-reduce | flops 256 | bytes 2048 | tf_op jit(solution)/shard_map/psum | solution.py:182
  206.6 176.9 %all-reduce.30.cloned.1.call-done = f32[3,3,256,256]{3,2,1,0:T(8,128)} async-done(((f32[3,3,256,256]{3,2,1,0:T(8,128)}), f32[3,3,256,256]{3,2,1,0:T(8,128)}) %all-reduce.30.cloned.1.call-update) | async-done | bytes 2359312 | tf_op jit(solution)/shard_map/psum | solution.py:182
  383.6 3.2 copy.91
  (229 shorter events, 24.1 us)
Async XLA Ops:
  7.2 8.0 %copy-start = (s32[1,2,16,2]{2,3,1,0:T(2,128)S(1)}, s32[1,2,16,2]{2,3,1,0:T(2,128)}, u32[]{:S(2)}) copy-start(s32[1,2,16,2]{2,3,1,0:T(2,128)} %param.32) | copy-start | bytes 772
  7.2 376.4 %all-reduce.30.cloned.1.call-start = ((), (), s32[]{:S(2)}) async-start(), calls=%async_computation | async-start | bytes 4718592 | tf_op jit(solution)/shard_map/psum | solution.py:182
  8.0 7.2 %collective-permute-start = (bf16[1,2,1,32,256]{4,3,2,1,0:T(8,128)(2,1)S(1)}, bf16[1,2,1,32,256]{4,3,2,1,0:T(8,128)(2,1)S(1)}, u32[]{:S(2)}, u32[]{:S(2)}) collective-permute-start(bf16[1,2,1,32,256]{4,3,2,1,0:T(8,128)(2,1)S(1)} %get-tuple-element.180), channel_id=1, source_target_pairs={{0,64},{64,128},{128,192},{1,65},{65,129},{129,193},{2,66},{66,130... | collective-permute-start | bytes 98312 | tf_op jit(solution)/shard_map/ppermute | solution.py:19
  11.4 5.8 %collective-permute-start.1 = (bf16[1,2,1,32,256]{4,3,2,1,0:T(8,128)(2,1)S(1)}, bf16[1,2,1,32,256]{4,3,2,1,0:T(8,128)(2,1)S(1)}, u32[]{:S(2)}, u32[]{:S(2)}) collective-permute-start(bf16[1,2,1,32,256]{4,3,2,1,0:T(8,128)(2,1)S(1)} %get-tuple-element.179), channel_id=1, source_target_pairs={{64,0},{128,64},{192,128},{65,1},{129,65},{193,129},{66,2},{130,66... | collective-permute-start | bytes 98312 | tf_op jit(solution)/shard_map/ppermute | solution.py:21
  17.3 15.5 %collective-permute-start.2 = (bf16[1,2,18,1,256]{4,3,2,1,0:T(2,128)(2,1)S(1)}, bf16[1,2,18,1,256]{4,3,2,1,0:T(2,128)(2,1)S(1)}, u32[]{:S(2)}, u32[]{:S(2)}) collective-permute-start(bf16[1,2,18,1,256]{4,3,2,1,0:T(2,128)(2,1)S(1)} %get-tuple-element.176), channel_id=1, source_target_pairs={{0,4},{4,8},{8,12},{12,16},{16,20},{20,24},{24,28},{28,32},{32,36}... | collective-permute-start | bytes 55304 | tf_op jit(solution)/shard_map/ppermute | solution.py:19
  21.1 11.6 %collective-permute-start.3 = (bf16[1,2,18,1,256]{4,3,2,1,0:T(2,128)(2,1)S(1)}, bf16[1,2,18,1,256]{4,3,2,1,0:T(2,128)(2,1)S(1)}, u32[]{:S(2)}, u32[]{:S(2)}) collective-permute-start(bf16[1,2,18,1,256]{4,3,2,1,0:T(2,128)(2,1)S(1)} %get-tuple-element.177), channel_id=1, source_target_pairs={{4,0},{8,4},{12,8},{16,12},{20,16},{24,20},{28,24},{32,28},{36,32}... | collective-permute-start | bytes 55304 | tf_op jit(solution)/shard_map/ppermute | solution.py:21
  24.5 14.8 %copy-start.10 = (bf16[16,32,41]{2,1,0:T(8,128)(2,1)}, bf16[16,32,41]{2,1,0:T(8,128)(2,1)S(1)}, u32[]{:S(2)}) copy-start(bf16[16,32,41]{2,1,0:T(8,128)(2,1)S(1)} %reshape.637) | copy-start | bytes 125956
  25.3 14.3 %copy-start.6 = (bf16[16,32,41]{2,1,0:T(8,128)(2,1)}, bf16[16,32,41]{2,1,0:T(8,128)(2,1)S(1)}, u32[]{:S(2)}) copy-start(bf16[16,32,41]{2,1,0:T(8,128)(2,1)S(1)} %reshape.639) | copy-start | bytes 125956
  26.1 13.9 %copy-start.8 = (bf16[16,32,41]{2,1,0:T(8,128)(2,1)}, bf16[16,32,41]{2,1,0:T(8,128)(2,1)S(1)}, u32[]{:S(2)}) copy-start(bf16[16,32,41]{2,1,0:T(8,128)(2,1)S(1)} %reshape.641) | copy-start | bytes 125956
  26.9 13.4 %copy-start.12 = (bf16[16,32,41]{2,1,0:T(8,128)(2,1)}, bf16[16,32,41]{2,1,0:T(8,128)(2,1)S(1)}, u32[]{:S(2)}) copy-start(bf16[16,32,41]{2,1,0:T(8,128)(2,1)S(1)} %reshape.643) | copy-start | bytes 125956
  27.7 12.9 %copy-start.14 = (bf16[16,32,41]{2,1,0:T(8,128)(2,1)}, bf16[16,32,41]{2,1,0:T(8,128)(2,1)S(1)}, u32[]{:S(2)}) copy-start(bf16[16,32,41]{2,1,0:T(8,128)(2,1)S(1)} %reshape.645) | copy-start | bytes 125956
  28.5 12.4 %copy-start.16 = (bf16[16,32,41]{2,1,0:T(8,128)(2,1)}, bf16[16,32,41]{2,1,0:T(8,128)(2,1)S(1)}, u32[]{:S(2)}) copy-start(bf16[16,32,41]{2,1,0:T(8,128)(2,1)S(1)} %reshape.647) | copy-start | bytes 125956
  29.3 12.0 %copy-start.18 = (bf16[16,32,41]{2,1,0:T(8,128)(2,1)}, bf16[16,32,41]{2,1,0:T(8,128)(2,1)S(1)}, u32[]{:S(2)}) copy-start(bf16[16,32,41]{2,1,0:T(8,128)(2,1)S(1)} %reshape.649) | copy-start | bytes 125956
  30.1 11.5 %copy-start.20 = (bf16[16,32,41]{2,1,0:T(8,128)(2,1)}, bf16[16,32,41]{2,1,0:T(8,128)(2,1)S(1)}, u32[]{:S(2)}) copy-start(bf16[16,32,41]{2,1,0:T(8,128)(2,1)S(1)} %reshape.651) | copy-start | bytes 125956
  33.3 1.7 copy-start.3
  37.4 0.7 copy-start.31
  38.2 0.8 copy-start.1
  53.0 6.4 %copy-start.4 = (bf16[3,3,256,256]{3,2,1,0:T(8,128)(2,1)S(1)}, bf16[3,3,256,256]{3,2,1,0:T(8,128)(2,1)}, u32[]{:S(2)}) copy-start(bf16[3,3,256,256]{3,2,1,0:T(8,128)(2,1)} %param.33) | copy-start | bytes 3538948
  53.0 6.4 %copy-start.5 = (f32[512,256]{1,0:T(8,128)S(1)}, f32[512,256]{1,0:T(8,128)}, u32[]{:S(2)}) copy-start(f32[512,256]{1,0:T(8,128)} %fusion.79) | copy-start | bytes 1572868
  53.0 6.4 %copy-start.30 = (bf16[16,32,256]{2,1,0:T(8,128)(2,1)S(1)}, bf16[16,32,256]{2,1,0:T(8,128)(2,1)}, u32[]{:S(2)}) copy-start(bf16[16,32,256]{2,1,0:T(8,128)(2,1)} %get-tuple-element.190) | copy-start | bytes 786436
  53.0 6.7 %copy-start.29 = (bf16[16,32,256]{2,1,0:T(8,128)(2,1)S(1)}, bf16[16,32,256]{2,1,0:T(8,128)(2,1)}, u32[]{:S(2)}) copy-start(bf16[16,32,256]{2,1,0:T(8,128)(2,1)} %get-tuple-element.189) | copy-start | bytes 786436
  53.1 6.8 %copy-start.28 = (bf16[16,32,256]{2,1,0:T(8,128)(2,1)S(1)}, bf16[16,32,256]{2,1,0:T(8,128)(2,1)}, u32[]{:S(2)}) copy-start(bf16[16,32,256]{2,1,0:T(8,128)(2,1)} %get-tuple-element.188) | copy-start | bytes 786436
  53.2 7.0 %copy-start.27 = (bf16[16,32,256]{2,1,0:T(8,128)(2,1)S(1)}, bf16[16,32,256]{2,1,0:T(8,128)(2,1)}, u32[]{:S(2)}) copy-start(bf16[16,32,256]{2,1,0:T(8,128)(2,1)} %get-tuple-element.187) | copy-start | bytes 786436
  53.2 9.9 %collective-permute-start.8 = (bf16[12,56,256]{2,1,0:T(8,128)(2,1)S(1)}, bf16[12,56,256]{2,1,0:T(8,128)(2,1)S(1)}, u32[]{:S(2)}, u32[]{:S(2)}) collective-permute-start(bf16[12,56,256]{2,1,0:T(8,128)(2,1)S(1)} %get-tuple-element.170), channel_id=1, source_target_pairs={{0,64},{64,128},{128,192},{1,65},{65,129},{129,193},{2,66},{66,130... | collective-permute-start | bytes 1032200 | tf_op jit(solution)/shard_map/ppermute | solution.py:19
  56.2 9.3 %collective-permute-start.9 = (bf16[12,56,256]{2,1,0:T(8,128)(2,1)S(1)}, bf16[12,56,256]{2,1,0:T(8,128)(2,1)S(1)}, u32[]{:S(2)}, u32[]{:S(2)}) collective-permute-start(bf16[12,56,256]{2,1,0:T(8,128)(2,1)S(1)} %get-tuple-element.171), channel_id=1, source_target_pairs={{64,0},{128,64},{192,128},{65,1},{129,65},{193,129},{66,2},{130,66... | collective-permute-start | bytes 1032200 | tf_op jit(solution)/shard_map/ppermute | solution.py:21
  59.7 1.0 copy-start.26
  59.9 1.0 copy-start.25
  60.6 1.0 copy-start.24
  65.6 6.9 %copy-start.23 = (bf16[16,32,256]{2,1,0:T(8,128)(2,1)S(1)}, bf16[16,32,256]{2,1,0:T(8,128)(2,1)}, u32[]{:S(2)}) copy-start(bf16[16,32,256]{2,1,0:T(8,128)(2,1)} %get-tuple-element.183) | copy-start | bytes 786436
  65.9 7.9 %collective-permute-start.10 = (bf16[16,12,256]{2,1,0:T(8,128)(2,1)S(1)}, bf16[16,12,256]{2,1,0:T(8,128)(2,1)S(1)}, u32[]{:S(2)}, u32[]{:S(2)}) collective-permute-start(bf16[16,12,256]{2,1,0:T(8,128)(2,1)S(1)} %get-tuple-element.181), channel_id=1, source_target_pairs={{0,4},{4,8},{8,12},{12,16},{16,20},{20,24},{24,28},{28,32},{32,36}... | collective-permute-start | bytes 294920 | tf_op jit(solution)/shard_map/ppermute | solution.py:19
  71.3 6.9 %collective-permute-start.11 = (bf16[16,12,256]{2,1,0:T(8,128)(2,1)S(1)}, bf16[16,12,256]{2,1,0:T(8,128)(2,1)S(1)}, u32[]{:S(2)}, u32[]{:S(2)}) collective-permute-start(bf16[16,12,256]{2,1,0:T(8,128)(2,1)S(1)} %get-tuple-element.182), channel_id=1, source_target_pairs={{4,0},{8,4},{12,8},{16,12},{20,16},{24,20},{28,24},{32,28},{36,32}... | collective-permute-start | bytes 294920 | tf_op jit(solution)/shard_map/ppermute | solution.py:21
  79.2 9.9 %collective-permute-start.4 = (bf16[12,32,256]{2,1,0:T(8,128)(2,1)S(1)}, bf16[12,32,256]{2,1,0:T(8,128)(2,1)S(1)}, u32[]{:S(2)}, u32[]{:S(2)}) collective-permute-start(bf16[12,32,256]{2,1,0:T(8,128)(2,1)S(1)} %get-tuple-element.210), channel_id=1, source_target_pairs={{0,64},{64,128},{128,192},{1,65},{65,129},{129,193},{2,66},{66,130... | collective-permute-start | bytes 589832 | tf_op jit(solution)/shard_map/ppermute | solution.py:19
  82.3 7.6 %collective-permute-start.5 = (bf16[12,32,256]{2,1,0:T(8,128)(2,1)S(1)}, bf16[12,32,256]{2,1,0:T(8,128)(2,1)S(1)}, u32[]{:S(2)}, u32[]{:S(2)}) collective-permute-start(bf16[12,32,256]{2,1,0:T(8,128)(2,1)S(1)} %get-tuple-element.211), channel_id=1, source_target_pairs={{64,0},{128,64},{192,128},{65,1},{129,65},{193,129},{66,2},{130,66... | collective-permute-start | bytes 589832 | tf_op jit(solution)/shard_map/ppermute | solution.py:21
  90.0 16.2 %copy-start.11 = (bf16[16,32,41]{2,1,0:T(8,128)(2,1)S(1)}, bf16[16,32,41]{2,1,0:T(8,128)(2,1)}, u32[]{:S(2)}) copy-start(bf16[16,32,41]{2,1,0:T(8,128)(2,1)} %copy-done.10) | copy-start | bytes 125956
  90.1 9.3 %collective-permute-start.6 = (bf16[40,12,256]{2,1,0:T(8,128)(2,1)S(1)}, bf16[40,12,256]{2,1,0:T(8,128)(2,1)S(1)}, u32[]{:S(2)}, u32[]{:S(2)}) collective-permute-start(bf16[40,12,256]{2,1,0:T(8,128)(2,1)S(1)} %get-tuple-element.175), channel_id=1, source_target_pairs={{0,4},{4,8},{8,12},{12,16},{16,20},{20,24},{24,28},{28,32},{32,36}... | collective-permute-start | bytes 737288 | tf_op jit(solution)/shard_map/ppermute | solution.py:19
  94.8 10.0 %collective-permute-start.7 = (bf16[40,12,256]{2,1,0:T(8,128)(2,1)S(1)}, bf16[40,12,256]{2,1,0:T(8,128)(2,1)S(1)}, u32[]{:S(2)}, u32[]{:S(2)}) collective-permute-start(bf16[40,12,256]{2,1,0:T(8,128)(2,1)S(1)} %get-tuple-element.174), channel_id=1, source_target_pairs={{4,0},{8,4},{12,8},{16,12},{20,16},{24,20},{28,24},{32,28},{36,32}... | collective-permute-start | bytes 737288 | tf_op jit(solution)/shard_map/ppermute | solution.py:21
  108.2 1.1 copy-start.7
  108.7 0.9 copy-start.9
  109.1 0.9 copy-start.13
  109.4 0.9 copy-start.15
  109.6 0.9 copy-start.17
  110.1 0.9 copy-start.19
  110.3 1.1 copy-start.2
  110.3 1.1 copy-start.21
  115.9 0.9 copy-start.22
Sparse Core Ops, SparseCore 0:
  116.1 267.4 all-reduce.29
where the time goes:
time: 395 us; the launch traced here: 394 us
  waiting for transfers between devices  196 us (50%)
  blocking collectives  82.2 us (21%)
  local copies, waits for them, and re-layouts  37.2 us (9%)
  starting transfers between devices  35.7 us (9%)
  matrix products  19.2 us (5%)
  between operations  18.2 us (5%)
  other arithmetic  5.36 us (1%)
    psum x1, waiting for transfers between devices, shards(): grad_w, grad_b = lax.psum((grad_w, grad_b), ('row', 'col', 'pair'))  177 us
    psum x1, blocking collectives, shards(): grad_w, grad_b = lax.psum((grad_w, grad_b), ('row', 'col', 'pair'))  82.2 us
    ppermute x6, starting transfers between devices, with_halo(): lax.ppermute(tail, axis, [(i, (i + 1) % count) for i in range(ends)])  23.4 us
    ppermute x6, waiting for transfers between devices, with_halo(): lax.ppermute(head, axis, [((i + 1) % count, i) for i in range(ends)])  13.9 us
    ppermute x6, starting transfers between devices, with_halo(): lax.ppermute(head, axis, [((i + 1) % count, i) for i in range(ends)])  12.2 us
    unnamed x86, local copies, waits for them, and re-layouts  11.7 us
    dynamic_update_slice x1, local copies, waits for them, and re-layouts, shards(): lax.dynamic_update_slice(gradient_second_padded, grad_window * inv_root,...  9.84 us
  transfers between devices with their start and end apart: 13, of which 9 were waited for; matrix products, arithmetic and copies ran while one was open for 6% of the time, Pallas kernels for 0%

commit v1 on v0

--- a/solution.py
+++ b/solution.py
@@ -179,7 +179,7 @@
     delta_one = jnp.where(pre_one > 0, grad_pieces, 0.0).astype(jnp.bfloat16)
     grad_w = weight_terms(first_pad, delta_one, False) + weight_terms(second_pad, delta_two, True)
     grad_b = jnp.sum(delta_one.astype(jnp.float32), axis=(0, 1)) + jnp.sum(delta_two, axis=(0, 1))
-    grad_w, grad_b = lax.psum((grad_w, grad_b), ("row", "col", "pair"))
+    grad_w, grad_b = lax.psum(lax.psum((grad_w, grad_b), ("col", "pair")), "row")
     return (corr, grad_w, grad_b)
 
 

time: 395 us -> 463 us (1.17)
  blocking collectives: 82.2 us -> 137 us
  waiting for transfers between devices: 196 us -> 208 us
    psum x1 -> x2, blocking collectives: 82.2 us -> 137 us  [the longest x1 128 us: shards(): lax.psum((grad_w, grad_b), ('col', 'pair'))]
    psum x1 -> x2, waiting for transfers between devices: 177 us -> 190 us  [the longest x1 190 us: shards(): lax.psum((grad_w, grad_b), ('col', 'pair'))]
    unnamed x86 -> x90, local copies, waits for them, and re-layouts: 11.7 us -> 11.3 us
  transfers between devices with their start and end apart: 13 -> 14, of which waited for: 9 -> 9; matrix products, arithmetic and copies ran while one was open for 6% -> 5% of each run, Pallas kernels for 0% -> 0%
where the time goes in v1:
time: 463 us; the launch traced here: 462 us
  waiting for transfers between devices  208 us (45%)
  blocking collectives  137 us (30%)
  local copies, waits for them, and re-layouts  37.6 us (8%)
  starting transfers between devices  36.2 us (8%)
  matrix products  19.2 us (4%)
  between operations  18.2 us (4%)
  other arithmetic  5.35 us (1%)
    psum x1, waiting for transfers between devices, shards(): lax.psum((grad_w, grad_b), ('col', 'pair'))  190 us
    psum x1, blocking collectives, shards(): lax.psum((grad_w, grad_b), ('col', 'pair'))  128 us
    ppermute x6, starting transfers between devices, with_halo(): lax.ppermute(tail, axis, [(i, (i + 1) % count) for i in range(ends)])  23.4 us
    ppermute x6, waiting for transfers between devices, with_halo(): lax.ppermute(head, axis, [((i + 1) % count, i) for i in range(ends)])  13.9 us
    ppermute x6, starting transfers between devices, with_halo(): lax.ppermute(head, axis, [((i + 1) % count, i) for i in range(ends)])  12.4 us
    unnamed x90, local copies, waits for them, and re-layouts  11.3 us
    dynamic_update_slice x1, local copies, waits for them, and re-layouts, shards(): lax.dynamic_update_slice(gradient_second_padded, grad_window * inv_root,...  9.84 us
  transfers between devices with their start and end apart: 14, of which 9 were waited for; matrix products, arithmetic and copies ran while one was open for 5% of the time, Pallas kernels for 0%

profile of v1, /device:TPU:2, one launch (start us, length us, event | category | flops | bytes accessed | tf_op | source)
XLA Modules:
  0.0 461.6 jit_solution(6530025373066683666)
XLA Ops:
  7.2 0.8 fusion.142
  8.0 3.4 collective-permute-start
  11.4 2.4 collective-permute-start.1
  13.9 1.2 copy.31
  15.3 1.1 constant_dynamic-update-slice_fusion.1
  16.3 0.9 collective-permute-done.1
  17.3 3.8 collective-permute-start.2
  21.1 1.3 collective-permute-start.3
  22.4 0.5 fusion.147
  23.4 0.3 reshape.635
  24.2 0.3 reshape.637
  25.0 0.3 reshape.639
  25.8 0.3 reshape.641
  26.6 0.3 reshape.643
  27.4 0.3 reshape.645
  28.2 0.3 reshape.647
  29.0 0.3 reshape.649
  29.8 0.3 reshape.651
  32.8 0.4 pad_maximum_fusion
  33.3 1.6 fusion.144
  34.9 1.1 fusion.79
  38.2 0.7 copy-done.2
  40.6 0.3 fusion.3
  40.9 0.3 fusion.2
  41.3 0.3 fusion.1
  41.9 1.0 broadcast_multiply_fusion
  43.1 9.8 %dynamic_update_slice.3 = f32[40,56,256]{2,1,0:T(8,128)S(1)} dynamic-update-slice(f32[40,56,256]{2,1,0:T(8,128)S(1)} %broadcast_in_dim.4, f32[24,40,256]{2,1,0:T(8,128)} %broadcast_multiply_fusion, s32[]{:T(128)S(6)} %select_n.33, s32[]{:T(128)S(6)} %select_n.34, s32[]{:T(128)} %constant.386.clone.1) | dynamic-update-slice | bytes 1966084 | tf_op jit(solution)/shard_map/dynamic_update_slice | solution.py:154
  53.2 3.0 collective-permute-start.8
  56.2 3.2 collective-permute-start.9
  61.1 0.4 copy-done.25
  61.8 1.3 collective-permute-done.8
  63.1 2.4 collective-permute-done.9
  65.8 5.4 %collective-permute-start.10 = (bf16[16,12,256]{2,1,0:T(8,128)(2,1)S(1)}, bf16[16,12,256]{2,1,0:T(8,128)(2,1)S(1)}, u32[]{:S(2)}, u32[]{:S(2)}) collective-permute-start(bf16[16,12,256]{2,1,0:T(8,128)(2,1)S(1)} %get-tuple-element.181), channel_id=1, source_target_pairs={{0,4},{4,8},{8,12},{12,16},{16,20},{20,24},{24,28},{28,32},{32,36}... | collective-permute-start | bytes 294920 | tf_op jit(solution)/shard_map/ppermute | solution.py:19
  71.2 1.3 collective-permute-start.11
  72.8 0.9 collective-permute-done.10
  73.7 4.4 collective-permute-done.11
  78.2 0.4 scatter-add.61
  78.6 0.3 scatter-add.64
  79.2 3.1 collective-permute-start.4
  82.3 2.7 collective-permute-start.5
  85.0 0.5 fusion.19
  85.5 0.5 fusion.18
  86.0 0.5 fusion.17
  86.5 0.5 fusion.16
  87.0 0.5 fusion.15
  87.5 0.5 fusion.14
  88.0 0.5 fusion.13
  88.5 0.5 fusion.12
  89.0 0.8 collective-permute-done.5
  90.0 4.7 %collective-permute-start.6 = (bf16[40,12,256]{2,1,0:T(8,128)(2,1)S(1)}, bf16[40,12,256]{2,1,0:T(8,128)(2,1)S(1)}, u32[]{:S(2)}, u32[]{:S(2)}) collective-permute-start(bf16[40,12,256]{2,1,0:T(8,128)(2,1)S(1)} %get-tuple-element.175), channel_id=1, source_target_pairs={{0,4},{4,8},{8,12},{12,16},{16,20},{20,24},{24,28},{28,32},{32,36}... | collective-permute-start | bytes 737288 | tf_op jit(solution)/shard_map/ppermute | solution.py:19
  94.8 1.5 collective-permute-start.7
  96.3 0.5 fusion.11
  96.8 2.5 collective-permute-done.6
  99.3 5.5 %collective-permute-done.7 = bf16[40,12,256]{2,1,0:T(8,128)(2,1)S(1)} collective-permute-done((bf16[40,12,256]{2,1,0:T(8,128)(2,1)S(1)}, bf16[40,12,256]{2,1,0:T(8,128)(2,1)S(1)}, u32[]{:S(2)}, u32[]{:S(2)}) %collective-permute-start.7) | collective-permute-done | bytes 245792 | tf_op jit(solution)/shard_map/ppermute | solution.py:21
  104.8 1.4 fusion.32
  106.3 0.9 fusion.39
  113.7 1.7 add.335
  115.8 0.6 copy-done.23
  119.7 1.0 reshape.619
  120.9 189.6 %all-reduce.31.cloned.1.call-done = f32[3,3,256,256]{3,2,1,0:T(8,128)} async-done(((f32[3,3,256,256]{3,2,1,0:T(8,128)}), f32[3,3,256,256]{3,2,1,0:T(8,128)}) %all-reduce.31.cloned.1.call-update) | async-done | bytes 2359312 | tf_op jit(solution)/shard_map/psum | solution.py:182
  313.8 1.0 copy.41
  314.8 127.5 %psum.30 = f32[256]{0:T(256)S(1)} all-reduce(f32[256]{0:T(256)S(1)} %add.337), channel_id=1, replica_groups=mesh['row'=4,'col'=16,'pair'=4] {'col','pair'}, use_global_device_ids=true, to_apply=%region_4.5 | all-reduce | flops 256 | bytes 2048 | tf_op jit(solution)/shard_map/psum | solution.py:182
  442.4 9.2 %psum.31 = f32[256]{0:T(256)} all-reduce(f32[256]{0:T(256)S(1)} %psum.30), channel_id=1, replica_groups=mesh['row'=4,'col'=16,'pair'=4] {'row'}, use_global_device_ids=true, to_apply=%region_5.6 | all-reduce | flops 256 | bytes 2048 | tf_op jit(solution)/shard_map/psum | solution.py:182
  451.5 3.2 copy.92
  (237 shorter events, 24.7 us)
Async XLA Ops:
  7.2 8.0 %copy-start = (s32[1,2,16,2]{2,3,1,0:T(2,128)S(1)}, s32[1,2,16,2]{2,3,1,0:T(2,128)}, u32[]{:S(2)}) copy-start(s32[1,2,16,2]{2,3,1,0:T(2,128)} %param.32) | copy-start | bytes 772
  7.2 303.3 %all-reduce.31.cloned.1.call-start = ((), (), s32[]{:S(2)}) async-start(), calls=%async_computation | async-start | bytes 4718592 | tf_op jit(solution)/shard_map/psum | solution.py:182
  8.0 7.2 %collective-permute-start = (bf16[1,2,1,32,256]{4,3,2,1,0:T(8,128)(2,1)S(1)}, bf16[1,2,1,32,256]{4,3,2,1,0:T(8,128)(2,1)S(1)}, u32[]{:S(2)}, u32[]{:S(2)}) collective-permute-start(bf16[1,2,1,32,256]{4,3,2,1,0:T(8,128)(2,1)S(1)} %get-tuple-element.180), channel_id=1, source_target_pairs={{0,64},{64,128},{128,192},{1,65},{65,129},{129,193},{2,66},{66,130... | collective-permute-start | bytes 98312 | tf_op jit(solution)/shard_map/ppermute | solution.py:19
  11.4 5.8 %collective-permute-start.1 = (bf16[1,2,1,32,256]{4,3,2,1,0:T(8,128)(2,1)S(1)}, bf16[1,2,1,32,256]{4,3,2,1,0:T(8,128)(2,1)S(1)}, u32[]{:S(2)}, u32[]{:S(2)}) collective-permute-start(bf16[1,2,1,32,256]{4,3,2,1,0:T(8,128)(2,1)S(1)} %get-tuple-element.179), channel_id=1, source_target_pairs={{64,0},{128,64},{192,128},{65,1},{129,65},{193,129},{66,2},{130,66... | collective-permute-start | bytes 98312 | tf_op jit(solution)/shard_map/ppermute | solution.py:21
  17.3 15.5 %collective-permute-start.2 = (bf16[1,2,18,1,256]{4,3,2,1,0:T(2,128)(2,1)S(1)}, bf16[1,2,18,1,256]{4,3,2,1,0:T(2,128)(2,1)S(1)}, u32[]{:S(2)}, u32[]{:S(2)}) collective-permute-start(bf16[1,2,18,1,256]{4,3,2,1,0:T(2,128)(2,1)S(1)} %get-tuple-element.176), channel_id=1, source_target_pairs={{0,4},{4,8},{8,12},{12,16},{16,20},{20,24},{24,28},{28,32},{32,36}... | collective-permute-start | bytes 55304 | tf_op jit(solution)/shard_map/ppermute | solution.py:19
  21.1 11.6 %collective-permute-start.3 = (bf16[1,2,18,1,256]{4,3,2,1,0:T(2,128)(2,1)S(1)}, bf16[1,2,18,1,256]{4,3,2,1,0:T(2,128)(2,1)S(1)}, u32[]{:S(2)}, u32[]{:S(2)}) collective-permute-start(bf16[1,2,18,1,256]{4,3,2,1,0:T(2,128)(2,1)S(1)} %get-tuple-element.177), channel_id=1, source_target_pairs={{4,0},{8,4},{12,8},{16,12},{20,16},{24,20},{28,24},{32,28},{36,32}... | collective-permute-start | bytes 55304 | tf_op jit(solution)/shard_map/ppermute | solution.py:21
  24.5 14.8 %copy-start.9 = (bf16[16,32,41]{2,1,0:T(8,128)(2,1)}, bf16[16,32,41]{2,1,0:T(8,128)(2,1)S(1)}, u32[]{:S(2)}) copy-start(bf16[16,32,41]{2,1,0:T(8,128)(2,1)S(1)} %reshape.637) | copy-start | bytes 125956
  25.3 14.3 %copy-start.7 = (bf16[16,32,41]{2,1,0:T(8,128)(2,1)}, bf16[16,32,41]{2,1,0:T(8,128)(2,1)S(1)}, u32[]{:S(2)}) copy-start(bf16[16,32,41]{2,1,0:T(8,128)(2,1)S(1)} %reshape.639) | copy-start | bytes 125956
  26.1 13.8 %copy-start.11 = (bf16[16,32,41]{2,1,0:T(8,128)(2,1)}, bf16[16,32,41]{2,1,0:T(8,128)(2,1)S(1)}, u32[]{:S(2)}) copy-start(bf16[16,32,41]{2,1,0:T(8,128)(2,1)S(1)} %reshape.641) | copy-start | bytes 125956
  26.9 13.3 %copy-start.13 = (bf16[16,32,41]{2,1,0:T(8,128)(2,1)}, bf16[16,32,41]{2,1,0:T(8,128)(2,1)S(1)}, u32[]{:S(2)}) copy-start(bf16[16,32,41]{2,1,0:T(8,128)(2,1)S(1)} %reshape.643) | copy-start | bytes 125956
  27.7 12.9 %copy-start.15 = (bf16[16,32,41]{2,1,0:T(8,128)(2,1)}, bf16[16,32,41]{2,1,0:T(8,128)(2,1)S(1)}, u32[]{:S(2)}) copy-start(bf16[16,32,41]{2,1,0:T(8,128)(2,1)S(1)} %reshape.645) | copy-start | bytes 125956
  28.5 12.4 %copy-start.17 = (bf16[16,32,41]{2,1,0:T(8,128)(2,1)}, bf16[16,32,41]{2,1,0:T(8,128)(2,1)S(1)}, u32[]{:S(2)}) copy-start(bf16[16,32,41]{2,1,0:T(8,128)(2,1)S(1)} %reshape.647) | copy-start | bytes 125956
  29.3 11.9 %copy-start.19 = (bf16[16,32,41]{2,1,0:T(8,128)(2,1)}, bf16[16,32,41]{2,1,0:T(8,128)(2,1)S(1)}, u32[]{:S(2)}) copy-start(bf16[16,32,41]{2,1,0:T(8,128)(2,1)S(1)} %reshape.649) | copy-start | bytes 125956
  30.1 11.4 %copy-start.21 = (bf16[16,32,41]{2,1,0:T(8,128)(2,1)}, bf16[16,32,41]{2,1,0:T(8,128)(2,1)S(1)}, u32[]{:S(2)}) copy-start(bf16[16,32,41]{2,1,0:T(8,128)(2,1)S(1)} %reshape.651) | copy-start | bytes 125956
  33.3 1.7 copy-start.4
  37.4 0.7 copy-start.33
  38.1 0.8 copy-start.2
  52.9 6.4 %copy-start.5 = (bf16[3,3,256,256]{3,2,1,0:T(8,128)(2,1)S(1)}, bf16[3,3,256,256]{3,2,1,0:T(8,128)(2,1)}, u32[]{:S(2)}) copy-start(bf16[3,3,256,256]{3,2,1,0:T(8,128)(2,1)} %param.33) | copy-start | bytes 3538948
  52.9 6.4 %copy-start.6 = (f32[512,256]{1,0:T(8,128)S(1)}, f32[512,256]{1,0:T(8,128)}, u32[]{:S(2)}) copy-start(f32[512,256]{1,0:T(8,128)} %fusion.79) | copy-start | bytes 1572868
  53.0 6.4 %copy-start.31 = (bf16[16,32,256]{2,1,0:T(8,128)(2,1)S(1)}, bf16[16,32,256]{2,1,0:T(8,128)(2,1)}, u32[]{:S(2)}) copy-start(bf16[16,32,256]{2,1,0:T(8,128)(2,1)} %get-tuple-element.190) | copy-start | bytes 786436
  53.0 6.7 %copy-start.30 = (bf16[16,32,256]{2,1,0:T(8,128)(2,1)S(1)}, bf16[16,32,256]{2,1,0:T(8,128)(2,1)}, u32[]{:S(2)}) copy-start(bf16[16,32,256]{2,1,0:T(8,128)(2,1)} %get-tuple-element.189) | copy-start | bytes 786436
  53.1 6.8 %copy-start.29 = (bf16[16,32,256]{2,1,0:T(8,128)(2,1)S(1)}, bf16[16,32,256]{2,1,0:T(8,128)(2,1)}, u32[]{:S(2)}) copy-start(bf16[16,32,256]{2,1,0:T(8,128)(2,1)} %get-tuple-element.188) | copy-start | bytes 786436
  53.2 7.0 %copy-start.28 = (bf16[16,32,256]{2,1,0:T(8,128)(2,1)S(1)}, bf16[16,32,256]{2,1,0:T(8,128)(2,1)}, u32[]{:S(2)}) copy-start(bf16[16,32,256]{2,1,0:T(8,128)(2,1)} %get-tuple-element.187) | copy-start | bytes 786436
  53.2 9.9 %collective-permute-start.8 = (bf16[12,56,256]{2,1,0:T(8,128)(2,1)S(1)}, bf16[12,56,256]{2,1,0:T(8,128)(2,1)S(1)}, u32[]{:S(2)}, u32[]{:S(2)}) collective-permute-start(bf16[12,56,256]{2,1,0:T(8,128)(2,1)S(1)} %get-tuple-element.170), channel_id=1, source_target_pairs={{0,64},{64,128},{128,192},{1,65},{65,129},{129,193},{2,66},{66,130... | collective-permute-start | bytes 1032200 | tf_op jit(solution)/shard_map/ppermute | solution.py:19
  56.2 9.3 %collective-permute-start.9 = (bf16[12,56,256]{2,1,0:T(8,128)(2,1)S(1)}, bf16[12,56,256]{2,1,0:T(8,128)(2,1)S(1)}, u32[]{:S(2)}, u32[]{:S(2)}) collective-permute-start(bf16[12,56,256]{2,1,0:T(8,128)(2,1)S(1)} %get-tuple-element.171), channel_id=1, source_target_pairs={{64,0},{128,64},{192,128},{65,1},{129,65},{193,129},{66,2},{130,66... | collective-permute-start | bytes 1032200 | tf_op jit(solution)/shard_map/ppermute | solution.py:21
  59.6 1.0 copy-start.27
  59.9 1.0 copy-start.26
  60.6 1.0 copy-start.25
  65.6 6.9 %copy-start.24 = (bf16[16,32,256]{2,1,0:T(8,128)(2,1)S(1)}, bf16[16,32,256]{2,1,0:T(8,128)(2,1)}, u32[]{:S(2)}) copy-start(bf16[16,32,256]{2,1,0:T(8,128)(2,1)} %get-tuple-element.183) | copy-start | bytes 786436
  65.8 7.9 %collective-permute-start.10 = (bf16[16,12,256]{2,1,0:T(8,128)(2,1)S(1)}, bf16[16,12,256]{2,1,0:T(8,128)(2,1)S(1)}, u32[]{:S(2)}, u32[]{:S(2)}) collective-permute-start(bf16[16,12,256]{2,1,0:T(8,128)(2,1)S(1)} %get-tuple-element.181), channel_id=1, source_target_pairs={{0,4},{4,8},{8,12},{12,16},{16,20},{20,24},{24,28},{28,32},{32,36}... | collective-permute-start | bytes 294920 | tf_op jit(solution)/shard_map/ppermute | solution.py:19
  71.2 6.9 %collective-permute-start.11 = (bf16[16,12,256]{2,1,0:T(8,128)(2,1)S(1)}, bf16[16,12,256]{2,1,0:T(8,128)(2,1)S(1)}, u32[]{:S(2)}, u32[]{:S(2)}) collective-permute-start(bf16[16,12,256]{2,1,0:T(8,128)(2,1)S(1)} %get-tuple-element.182), channel_id=1, source_target_pairs={{4,0},{8,4},{12,8},{16,12},{20,16},{24,20},{28,24},{32,28},{36,32}... | collective-permute-start | bytes 294920 | tf_op jit(solution)/shard_map/ppermute | solution.py:21
  79.2 9.9 %collective-permute-start.4 = (bf16[12,32,256]{2,1,0:T(8,128)(2,1)S(1)}, bf16[12,32,256]{2,1,0:T(8,128)(2,1)S(1)}, u32[]{:S(2)}, u32[]{:S(2)}) collective-permute-start(bf16[12,32,256]{2,1,0:T(8,128)(2,1)S(1)} %get-tuple-element.210), channel_id=1, source_target_pairs={{0,64},{64,128},{128,192},{1,65},{65,129},{129,193},{2,66},{66,130... | collective-permute-start | bytes 589832 | tf_op jit(solution)/shard_map/ppermute | solution.py:19
  82.3 7.6 %collective-permute-start.5 = (bf16[12,32,256]{2,1,0:T(8,128)(2,1)S(1)}, bf16[12,32,256]{2,1,0:T(8,128)(2,1)S(1)}, u32[]{:S(2)}, u32[]{:S(2)}) collective-permute-start(bf16[12,32,256]{2,1,0:T(8,128)(2,1)S(1)} %get-tuple-element.211), channel_id=1, source_target_pairs={{64,0},{128,64},{192,128},{65,1},{129,65},{193,129},{66,2},{130,66... | collective-permute-start | bytes 589832 | tf_op jit(solution)/shard_map/ppermute | solution.py:21
  89.9 16.2 %copy-start.10 = (bf16[16,32,41]{2,1,0:T(8,128)(2,1)S(1)}, bf16[16,32,41]{2,1,0:T(8,128)(2,1)}, u32[]{:S(2)}) copy-start(bf16[16,32,41]{2,1,0:T(8,128)(2,1)} %copy-done.9) | copy-start | bytes 125956
  90.0 9.3 %collective-permute-start.6 = (bf16[40,12,256]{2,1,0:T(8,128)(2,1)S(1)}, bf16[40,12,256]{2,1,0:T(8,128)(2,1)S(1)}, u32[]{:S(2)}, u32[]{:S(2)}) collective-permute-start(bf16[40,12,256]{2,1,0:T(8,128)(2,1)S(1)} %get-tuple-element.175), channel_id=1, source_target_pairs={{0,4},{4,8},{8,12},{12,16},{16,20},{20,24},{24,28},{28,32},{32,36}... | collective-permute-start | bytes 737288 | tf_op jit(solution)/shard_map/ppermute | solution.py:19
  94.8 10.0 %collective-permute-start.7 = (bf16[40,12,256]{2,1,0:T(8,128)(2,1)S(1)}, bf16[40,12,256]{2,1,0:T(8,128)(2,1)S(1)}, u32[]{:S(2)}, u32[]{:S(2)}) collective-permute-start(bf16[40,12,256]{2,1,0:T(8,128)(2,1)S(1)} %get-tuple-element.174), channel_id=1, source_target_pairs={{4,0},{8,4},{12,8},{16,12},{20,16},{24,20},{28,24},{32,28},{36,32}... | collective-permute-start | bytes 737288 | tf_op jit(solution)/shard_map/ppermute | solution.py:21
  107.7 1.1 copy-start.8
  108.2 0.9 copy-start.12
  108.7 0.9 copy-start.14
  108.9 0.9 copy-start.16
  109.1 0.9 copy-start.18
  109.6 0.9 copy-start.20
  109.8 1.1 copy-start.3
  109.8 1.1 copy-start.22
  115.4 0.9 copy-start.23
  115.5 336.0 %all-reduce.33.cloned.1.call-start = ((), (), s32[]{:S(2)}) async-start(), calls=%async_computation.1 | async-start | bytes 4718592 | tf_op jit(solution)/shard_map/psum | solution.py:182
  120.8 189.8 %copy-start.32 = (f32[16,32,42]{2,1,0:T(8,128)S(1)}, f32[16,32,42]{2,1,0:T(8,128)}, u32[]{:S(2)}) copy-start(f32[16,32,42]{2,1,0:T(8,128)} %reshape.619) | copy-start | bytes 258052
  442.4 12.4 %copy-start.1 = (s32[1,2,16,2]{2,3,1,0:T(2,128)S(1)}, s32[1,2,16,2]{2,3,1,0:T(2,128)}, u32[]{:S(2)}) copy-start(s32[1,2,16,2]{2,3,1,0:T(2,128)} %param.32) | copy-start | bytes 772
Sparse Core Ops, SparseCore 0:
  115.6 194.8 all-reduce.30
  312.9 65.6 all-reduce.32
